TPU v7x, 32 devices: a whole 2x2x4 slice. The times are simulated.
32 devices in a mesh: ctx: 8 (over z, x), head: 4 (over y, core).
Axes of the slice: x: 2, y: 2, z: 4, core: 2. Of those that a mesh axis runs over, the one named last changes fastest.
Arguments:
- queries: bfloat16 [4096, 4096], P('ctx', 'head'), may hold values from -5 to 5
- keys: bfloat16 [4096, 512], P('ctx', 'head'), may hold values from -5 to 5
- values: bfloat16 [4096, 512], P('ctx', 'head'), may hold values from -8 to 8
- feature_map: bfloat16 [4, 128, 16], P('head'), may hold values from -0.5 to 0.5
- out_proj: bfloat16 [4096, 8192], P('ctx', 'head'), may hold values from -0.09375 to 0.09375
- teacher: bfloat16 [4096, 8192], P('ctx', 'head'), may hold values from -16 to 16
Outputs:
- student_out: bfloat16 [4096, 8192], P('ctx', 'head')
- loss: float32 [], replicated
- feature_grad: float32 [4, 128, 16], P('head')
All inputs are finite; a program needn't handle non-finite values.
Results may differ from a plain program's by a relative error of at most 0.006.
Values may be sent and summed in bfloat16 or wider, within the bound.
A program may use at most 128 MiB of HBM per device.

v0:
```python
import math
import jax
import jax.numpy as jnp
from jax import lax
from jax.sharding import PartitionSpec as P

D = 8192
HEAD_DIM = 128
GROUP = 8
WIN = 64
exact_mode = lax.Precision.HIGHEST


def shifted(block, axis, distance):
    devices = range(lax.axis_size(axis))
    route = [(i - distance, i) for i in devices if i - distance in devices]
    return lax.ppermute(block, axis, route)


def taylor_square(features):
    feature_count = features.shape[-1]
    outer = features[..., :, None] * features[..., None, :]
    return outer.reshape(features.shape[:-1] + (feature_count * feature_count,))


def square_grad(grad_square, features):
    feature_count = features.shape[-1]
    matrix = grad_square.reshape(features.shape + (feature_count,))
    return jnp.einsum("...fh,...h->...f", matrix, features, precision=exact_mode) + jnp.einsum(
        "...hf,...h->...f", matrix, features, precision=exact_mode
    )


def masked_total(select, member):
    shaped = select.reshape((select.shape[0],) + (1,) * (member.ndim - 1))
    return jnp.sum(jnp.where(shaped, member, jnp.zeros_like(member)), axis=0)


def window_tiles(extended, tok_rows):
    tile_count = tok_rows // WIN
    first = extended[:tok_rows].reshape((tile_count, WIN) + extended.shape[1:])
    second = extended[WIN:].reshape((tile_count, WIN) + extended.shape[1:])
    return jnp.concatenate([first, second], 1)


def local(queries, keys, values, feature_map, out_proj, teacher):
    tok_rows = queries.shape[0]
    kv_groups = keys.shape[1] // HEAD_DIM
    ctx_count = lax.axis_size("ctx")
    ctx_index = lax.axis_index("ctx")
    query_heads = queries.reshape(tok_rows, kv_groups, GROUP, HEAD_DIM)
    key_heads = keys.reshape(tok_rows, kv_groups, HEAD_DIM)
    value_float = values.reshape(tok_rows, kv_groups, HEAD_DIM).astype(jnp.float32)
    query_features = jnp.einsum(
        "tgqe,gef->tgqf", query_heads, feature_map, preferred_element_type=jnp.float32
    )
    key_features = jnp.einsum(
        "tge,gef->tgf", key_heads, feature_map, preferred_element_type=jnp.float32
    )
    rim_rows = shifted(jnp.stack([keys[tok_rows - WIN :], values[tok_rows - WIN :]]), "ctx", 1)
    keys_ext = jnp.concatenate([rim_rows[0], keys], 0).reshape(tok_rows + WIN, kv_groups, HEAD_DIM)
    values_ext = jnp.concatenate([rim_rows[1], values], 0).reshape(
        tok_rows + WIN, kv_groups, HEAD_DIM
    )
    tile_count = tok_rows // WIN
    key_tiles = window_tiles(keys_ext, tok_rows)
    value_tiles = window_tiles(values_ext, tok_rows)
    query_tiles = query_heads.reshape(tile_count, WIN, kv_groups, GROUP, HEAD_DIM)
    scores = jnp.einsum(
        "ntgqe,nsge->ngqts", query_tiles, key_tiles, preferred_element_type=jnp.float32
    ) / math.sqrt(HEAD_DIM)
    tile_pos = lax.broadcasted_iota(jnp.int32, (tile_count, WIN, 2 * WIN), 0)
    query_pos = lax.broadcasted_iota(jnp.int32, (tile_count, WIN, 2 * WIN), 1)
    key_pos = lax.broadcasted_iota(jnp.int32, (tile_count, WIN, 2 * WIN), 2)
    distance = query_pos + WIN - key_pos
    allowed = (
        (distance >= 0)
        & (distance < WIN)
        & (ctx_index * tok_rows + tile_pos * WIN + key_pos - WIN >= 0)
    )
    allowed = allowed[:, None, None]
    scores = jnp.where(allowed, scores, -jnp.inf)
    row_max = jnp.max(scores, axis=-1, keepdims=True)
    weights = jnp.where(allowed, jnp.exp(scores - row_max), 0.0)
    attn_weights = (weights / jnp.sum(weights, axis=-1, keepdims=True)).astype(jnp.bfloat16)
    window_out = jnp.einsum(
        "ngqts,nsge->ntgqe", attn_weights, value_tiles, preferred_element_type=jnp.float32
    ).reshape(tok_rows, kv_groups, GROUP, HEAD_DIM)
    causal = lax.broadcasted_iota(jnp.int32, (tok_rows, tok_rows), 0) >= lax.broadcasted_iota(
        jnp.int32, (tok_rows, tok_rows), 1
    )
    qk_inner = (
        jnp.einsum("tgqf,sgf->gqts", query_features, key_features, precision=exact_mode) / 4.0
    )
    kernel = jnp.where(causal, 1.0 + qk_inner + 0.5 * qk_inner * qk_inner, 0.0)
    numerator = jnp.einsum("gqts,sge->tgqe", kernel, value_float, precision=exact_mode)
    denominator = jnp.transpose(jnp.sum(kernel, axis=-1), (2, 0, 1))
    key_square = taylor_square(key_features)
    own_square_v = jnp.einsum("sgk,sge->gke", key_square, value_float, precision=exact_mode)
    own_linear_v = jnp.einsum("sgf,sge->gfe", key_features, value_float, precision=exact_mode)
    own_values = jnp.sum(value_float, axis=0)
    own_square_k = jnp.sum(key_square, axis=0)
    own_linear_k = jnp.sum(key_features, axis=0)
    own_count = jnp.full((kv_groups,), float(tok_rows), jnp.float32)
    gathered = (
        lax.all_gather(own_square_v[None], "ctx", axis=0, tiled=True),
        lax.all_gather(own_linear_v[None], "ctx", axis=0, tiled=True),
        lax.all_gather(own_values[None], "ctx", axis=0, tiled=True),
        lax.all_gather(own_square_k[None], "ctx", axis=0, tiled=True),
        lax.all_gather(own_linear_k[None], "ctx", axis=0, tiled=True),
        lax.all_gather(own_count[None], "ctx", axis=0, tiled=True),
    )
    lower_select = jnp.arange(ctx_count) < ctx_index
    earlier = tuple((masked_total(lower_select, member) for member in gathered))
    past_square_v, past_linear_v, past_values, past_square_k, past_linear_k, past_count = earlier
    query_square = taylor_square(query_features)
    numerator = (
        numerator
        + jnp.einsum("tgqk,gke->tgqe", query_square, past_square_v, precision=exact_mode) / 32.0
        + jnp.einsum("tgqf,gfe->tgqe", query_features, past_linear_v, precision=exact_mode) / 4.0
        + past_values[None, :, None, :]
    )
    denominator = (
        denominator
        + jnp.einsum("tgqk,gk->tgq", query_square, past_square_k, precision=exact_mode) / 32.0
        + jnp.einsum("tgqf,gf->tgq", query_features, past_linear_k, precision=exact_mode) / 4.0
        + past_count[None, :, None]
    )
    linear_out = numerator / denominator[..., None]
    head_out = (
        (linear_out + window_out)
        .astype(jnp.bfloat16)
        .reshape(tok_rows, kv_groups * GROUP * HEAD_DIM)
    )
    all_heads = lax.all_gather(head_out, "head", axis=1, tiled=True)
    proj_full = lax.all_gather(out_proj, "ctx", axis=0, tiled=True)
    projected = jnp.dot(all_heads, proj_full, preferred_element_type=jnp.float32)
    student_out = projected.astype(jnp.bfloat16)
    residual = student_out.astype(jnp.float32) - teacher.astype(jnp.float32)
    total_rows = tok_rows * ctx_count
    loss_value = lax.psum(jnp.sum(residual * residual), ("ctx", "head")) / (total_rows * D)
    d_student = (2.0 * residual / total_rows).astype(jnp.bfloat16)
    head_terms = lax.dot_general(
        d_student, proj_full, (((1,), (1,)), ((), ())), preferred_element_type=jnp.float32
    )
    head_grad = (
        lax.psum_scatter(head_terms.astype(jnp.bfloat16), "head", scatter_dimension=1, tiled=True)
        .astype(jnp.float32)
        .reshape(tok_rows, kv_groups, GROUP, HEAD_DIM)
    )
    numerator_grad = head_grad / denominator[..., None]
    denominator_grad = -jnp.sum(head_grad * linear_out, axis=-1) / denominator
    kernel_grad = (
        jnp.einsum("tgqe,sge->gqts", numerator_grad, value_float, precision=exact_mode)
        + jnp.transpose(denominator_grad, (1, 2, 0))[..., None]
    )
    inner_grad = jnp.where(causal, kernel_grad * (1.0 + qk_inner), 0.0) / 4.0
    query_grad = jnp.einsum("gqts,sgf->tgqf", inner_grad, key_features, precision=exact_mode)
    key_grad = jnp.einsum("gqts,tgqf->sgf", inner_grad, query_features, precision=exact_mode)
    query_square_grad = (
        jnp.einsum("tgqe,gke->tgqk", numerator_grad, past_square_v, precision=exact_mode)
        + denominator_grad[..., None] * past_square_k[None, :, None, :]
    ) / 32.0
    query_grad = (
        query_grad
        + (
            jnp.einsum("tgqe,gfe->tgqf", numerator_grad, past_linear_v, precision=exact_mode)
            + denominator_grad[..., None] * past_linear_k[None, :, None, :]
        )
        / 4.0
        + square_grad(query_square_grad, query_features)
    )
    own_back_square = jnp.einsum(
        "tgqk,tgqe->gke", query_square, numerator_grad, precision=exact_mode
    )
    own_back_linear = jnp.einsum(
        "tgqf,tgqe->gfe", query_features, numerator_grad, precision=exact_mode
    )
    own_den_square = jnp.einsum(
        "tgqk,tgq->gk", query_square, denominator_grad, precision=exact_mode
    )
    own_den_linear = jnp.einsum(
        "tgqf,tgq->gf", query_features, denominator_grad, precision=exact_mode
    )
    gathered_back = (
        lax.all_gather(own_back_square[None], "ctx", axis=0, tiled=True),
        lax.all_gather(own_back_linear[None], "ctx", axis=0, tiled=True),
        lax.all_gather(own_den_square[None], "ctx", axis=0, tiled=True),
        lax.all_gather(own_den_linear[None], "ctx", axis=0, tiled=True),
    )
    upper_select = jnp.arange(ctx_count) > ctx_index
    later_sums = tuple((masked_total(upper_select, member) for member in gathered_back))
    later_square, later_linear, later_den_square, later_den_linear = later_sums
    key_square_grad = (
        jnp.einsum("gke,sge->sgk", later_square, value_float, precision=exact_mode)
        + later_den_square[None]
    ) / 32.0
    key_grad = (
        key_grad
        + (
            jnp.einsum("gfe,sge->sgf", later_linear, value_float, precision=exact_mode)
            + later_den_linear[None]
        )
        / 4.0
        + square_grad(key_square_grad, key_features)
    )
    own_grad = jnp.einsum(
        "tgqe,tgqf->gef", query_heads.astype(jnp.float32), query_grad, precision=exact_mode
    ) + jnp.einsum("tge,tgf->gef", key_heads.astype(jnp.float32), key_grad, precision=exact_mode)
    feature_grad = lax.psum(own_grad, "ctx")
    return (student_out, loss_value, feature_grad)


def solution(mesh):
    return jax.shard_map(
        local,
        mesh=mesh,
        in_specs=(
            P("ctx", "head"),
            P("ctx", "head"),
            P("ctx", "head"),
            P("head", None, None),
            P("ctx", "head"),
            P("ctx", "head"),
        ),
        out_specs=(P("ctx", "head"), P(), P("head", None, None)),
        check_vma=False,
    )
```

profile of v0, /device:TPU:0, one launch (start us, length us, event | category | flops | bytes accessed | tf_op | source)
XLA Modules:
  0.0 652.8 jit_solution(9237488309166573956)
XLA Ops:
  9.4 5.4 collective-permute-start
  16.7 1.9 fusion.107
  20.9 18.1 %all_gather.39 = f32[8,1,256]{2,1,0:T(1,128)S(1)} all-gather(f32[1,1,256]{2,1,0:T(1,128)S(1)} %broadcast_in_dim.148), channel_id=1, replica_groups=mesh['ctx'=8,'head'=4] {'ctx'}, dimensions={0}, use_global_device_ids=true | all-gather | bytes 9216 | tf_op jit(solution)/shard_map/all_gather | solution.py:109
  40.1 1.9 copy-done.2
  42.0 7.1 %fusion.108 = f32[1,512,8]{0,1,2:T(8,128)S(1)} fusion(f32[256,1,1]{0,1,2:T(1,128)S(1)} %bitcast.398, f32[512,8,256]{0,2,1:T(8,128)S(1)} %bitcast.367), kind=kOutput, calls=%fused_computation.168 | convolution fusion | flops 12582912 | bytes 4211712 | tf_op jit(solution)/shard_map/tgqk,gk->tgq/dot_general | solution.py:125
  53.9 18.1 %all-reduce.3 = (f32[128]{0:T(128)S(1)}, f32[8]{0:T(128)}) all-reduce(f32[128]{0:T(128)S(1)} %dynamic-update-slice, f32[8]{0:T(128)S(1)} %dynamic-update-slice.1), channel_id=5, replica_groups=mesh['ctx'=8,'head'=4] {'ctx'}, use_global_device_ids=true, to_apply=%add | all-reduce | flops 136 | bytes 1088
  72.8 3.4 fusion.89
  77.4 11.7 %fusion.7 = (f32[8,512]{1,0:T(8,128)S(1)}, f32[512,512,8]{1,0,2:T(8,128)}) fusion(pred[512,512]{0,1:T(8,128)(4,1)} %iota_compare_fusion, f32[512,8,16]{0,2,1:T(8,128)S(1)} %convolution_bitcast_fusion.2, f32[16,512]{1,0:T(8,128)} %copy-done.6), kind=kOutput, calls=%fused_computation.10 | convolution fusion | flops 417329152 | bytes 8962048 | tf_op jit(solution)/shard_map/tgqf,sgf->gqts/dot_general | solution.py:93
  89.8 31.0 %all-gather.1 = f32[128,128]{1,0:T(8,128)S(1)} all-gather(f32[16,128]{1,0:T(8,128)S(1)} %fusion.93), channel_id=3, replica_groups=mesh['ctx'=8,'head'=4] {'ctx'}, dimensions={0}, use_global_device_ids=true | all-gather | bytes 73728 | tf_op jit(solution)/shard_map/all_gather | solution.py:107
  120.9 3.2 fusion.80
  124.1 9.7 %fusion.5 = f32[8,512,128]{1,2,0:T(8,128)} fusion(f32[512,512,8]{1,0,2:T(8,128)} %get-tuple-element.13, pred[512,512]{0,1:T(8,128)(4,1)S(1)} %copy-done.17, bf16[512,128]{1,0:T(8,128)(2,1)S(1)} %copy-done.5), kind=kOutput, calls=%fused_computation.7 | convolution fusion | flops 3233808384 | bytes 10878976 | tf_op jit(solution)/shard_map/gqts,sge->tgqe/dot_general | solution.py:96
  135.2 18.2 %all-gather.8 = f32[8,1,128]{2,1,0:T(1,128)S(1)} all-gather(f32[1,1,128]{2,1,0:T(1,128)S(1)} %bitcast.399), channel_id=4, replica_groups=mesh['ctx'=8,'head'=4] {'ctx'}, dimensions={0}, use_global_device_ids=true | all-gather | bytes 4608 | tf_op jit(solution)/shard_map/all_gather | solution.py:108
  157.3 2.6 convolution_bitcast_fusion
  164.3 8.5 %add_convert_fusion = (bf16[512,1,8,128]{0,3,2,1:T(8,128)(2,1)}, f32[512,1,8,128]{0,3,2,1:T(8,128)}) fusion(f32[512,1,8,128]{0,3,2,1:T(8,128)} %copy.53, f32[512,8]{0,1:T(8,128)} %bitcast.390, f32[128]{0:T(128)S(1)} %copy-done.26, f32[128,512,8]{1,0,2:T(8,128)} %fusion.80, f32[512,8,256]{0,2,1:T(8,128)} %bitcast.368, ...), kind=kOutput, calls=%fused_computation.38 | convolution fusion | flops 1614807040 | bytes 13779456 | tf_op jit(solution)/shard_map/tgqk,gke->tgqe/dot_general | solution.py:119
  173.8 30.9 %all-gather.15.cloned.1.call-done = bf16[512,4096]{0,1:T(8,128)(2,1)} async-done(((bf16[512,1024]{0,1:T(8,128)(2,1)}), bf16[512,4096]{0,1:T(8,128)(2,1)}) %all-gather.15.cloned.1.call-update) | async-done | bytes 4194320 | tf_op jit(solution)/shard_map/all_gather | solution.py:135
  204.8 229.8 %all-gather.17.cloned.1.call-done = bf16[4096,2048]{1,0:T(8,128)(2,1)} async-done(((bf16[512,2048]{1,0:T(8,128)(2,1)}), bf16[4096,2048]{1,0:T(8,128)(2,1)}) %all-gather.17.cloned.1.call-update) | async-done | bytes 16777232 | tf_op jit(solution)/shard_map/all_gather | solution.py:136
  434.6 14.8 %multiply_reduce_fusion.2 = (f32[]{:T(128)}, bf16[512,2048]{1,0:T(8,128)(2,1)S(1)}) fusion(bf16[512,2048]{1,0:T(8,128)(2,1)S(1)} %copy-done.28, bf16[512,4096]{0,1:T(8,128)(2,1)} %all-gather.15.cloned.1.call-done, bf16[4096,2048]{1,0:T(8,128)(2,1)} %all-gather.17.cloned.1.call-done), kind=kOutput, calls=%fused_computation.16 | convolution fusion | flops 8596226048 | bytes 25165828 | tf_op jit(solution)/shard_map/dot_general | solution.py:137
  450.7 13.8 %convolution_convert_fusion = bf16[512,4096]{1,0:T(8,128)(2,1)} fusion(bf16[4096,2048]{1,0:T(8,128)(2,1)} %all-gather.17.cloned.1.call-done, bf16[512,2048]{1,0:T(8,128)(2,1)S(1)} %copy-done.28, bf16[512,2048]{1,0:T(8,128)(2,1)S(1)} %get-tuple-element.21), kind=kOutput, calls=%fused_computation.9 | convolution fusion | flops 8597274624 | bytes 25165824 | tf_op jit(solution)/shard_map/dot_general | solution.py:143
  466.0 39.3 %psum.14 = f32[]{:T(128)} all-reduce(f32[]{:T(128)} %get-tuple-element.20), channel_id=1, replica_groups=mesh['ctx'=8,'head'=4] {'ctx','head'}, use_global_device_ids=true, to_apply=%region_13.14 | all-reduce | flops 1 | bytes 8 | tf_op jit(solution)/shard_map/psum | solution.py:141
  505.9 2.1 reduce-scatter.2.cloned.1.call-done
  509.5 2.3 multiply_reduce_fusion.3
  512.3 3.3 convolution_bitcast_fusion.7
  516.1 4.3 convolution_bitcast_fusion.3
  520.4 20.5 %all-gather.9 = f32[8,1,256]{2,1,0:T(1,128)S(1)} all-gather(f32[1,1,256]{2,1,0:T(1,128)S(1)} %convolution_bitcast_fusion.7), channel_id=9, replica_groups=mesh['ctx'=8,'head'=4] {'ctx'}, dimensions={0}, use_global_device_ids=true | all-gather | bytes 9216 | tf_op jit(solution)/shard_map/all_gather | solution.py:188
  542.4 30.8 %all-gather.4 = f32[128,128]{1,0:T(8,128)S(1)} all-gather(f32[16,128]{1,0:T(8,128)S(1)} %convolution_bitcast_fusion.6), channel_id=6, replica_groups=mesh['ctx'=8,'head'=4] {'ctx'}, dimensions={0}, use_global_device_ids=true | all-gather | bytes 73728 | tf_op jit(solution)/shard_map/all_gather | solution.py:187
  573.6 17.3 %all-reduce.2 = f32[128]{0:T(128)S(1)} all-reduce(f32[128]{0:T(128)S(1)} %dynamic-update-slice.2), channel_id=7, replica_groups=mesh['ctx'=8,'head'=4] {'ctx'}, use_global_device_ids=true, to_apply=%add.2 | all-reduce | flops 128 | bytes 1024
  591.7 4.1 fusion.9
  597.8 2.2 fusion.38
  600.0 10.8 %fusion.3 = f32[8,512,512]{1,2,0:T(8,128)S(1)} fusion(f32[512,512,8]{1,0,2:T(8,128)S(1)} %bitcast.401, f32[8,512]{1,0:T(8,128)S(1)} %get-tuple-element.7, pred[512,512]{0,1:T(8,128)(4,1)S(1)} %copy-done.18, bf16[512,128]{1,0:T(8,128)(2,1)S(1)} %copy-done.5, f32[64,8,8,128]{3,2,1,0:T(8,128)S(1)} %bitcast.380, bf16[512,1024]{1,0:T(8,128)(2,1)S(1)} %copy-done.10), kind=kOutput, calls=%fused_computation.4 | convolution fusion | flops 3234856960 | bytes 20332544 | tf_op jit(solution)/shard_map/tgqe,sge->gqts/dot_general | solution.py:154
  610.8 4.0 fusion.31
  615.5 7.1 %convolution_bitcast_fusion.4 = f32[512,1,16]{0,2,1:T(8,128)S(1)} fusion(f32[512,8,16]{0,2,1:T(8,128)S(1)} %convolution_bitcast_fusion.2, f32[8,512,512]{1,2,0:T(8,128)S(1)} %fusion.3), kind=kOutput, calls=%fused_computation.65 | convolution fusion | flops 402653184 | bytes 8683520 | tf_op jit(solution)/shard_map/gqts,tgqf->sgf/dot_general | solution.py:159
  624.9 20.0 %psum.15 = f32[1,128,16]{1,2,0:T(8,128)} all-reduce(f32[1,128,16]{1,2,0:T(8,128)S(1)} %fusion.46), channel_id=1, replica_groups=mesh['ctx'=8,'head'=4] {'ctx'}, use_global_device_ids=true, to_apply=%region_20.21 | all-reduce | flops 2048 | bytes 16384 | tf_op jit(solution)/shard_map/psum | solution.py:210
  (138 shorter events, 37.7 us)
Async XLA Ops:
  7.2 7.7 %copy-start = (bf16[1,128,16]{1,2,0:T(8,128)(2,1)S(1)}, bf16[1,128,16]{1,2,0:T(8,128)(2,1)}, u32[]{:S(2)}) copy-start(bf16[1,128,16]{1,2,0:T(8,128)(2,1)} %param.9) | copy-start | bytes 12292
  7.2 12.8 %copy-start.5 = (bf16[512,128]{1,0:T(8,128)(2,1)S(1)}, bf16[512,128]{1,0:T(8,128)(2,1)}, u32[]{:S(2)}) copy-start(bf16[512,128]{1,0:T(8,128)(2,1)} %param.8) | copy-start | bytes 393220
  7.2 31.8 %copy-start.4 = (bf16[512,1024]{1,0:T(8,128)(2,1)S(1)}, bf16[512,1024]{1,0:T(8,128)(2,1)}, u32[]{:S(2)}) copy-start(bf16[512,1024]{1,0:T(8,128)(2,1)} %param.6) | copy-start | bytes 3145732
  7.2 155.7 %all-gather.19.cloned.1.call-start = ((), (), s32[]{:S(2)}) async-start(), calls=%async_computation.4 | async-start | bytes 1179648 | tf_op jit(solution)/shard_map/all_gather | solution.py:106
  9.4 145.0 %collective-permute-start = (bf16[2,64,128]{2,1,0:T(8,128)(2,1)}, bf16[2,64,128]{2,1,0:T(8,128)(2,1)}, u32[]{:S(2)}, u32[]{:S(2)}) collective-permute-start(bf16[2,64,128]{2,1,0:T(8,128)(2,1)} %pad_maximum_fusion.2), channel_id=1, source_target_pairs={{0,4},{4,8},{8,12},{12,16},{16,20},{20,24},{24,28},{1,5},{5,9},{9,... | collective-permute-start | bytes 98312 | tf_op jit(solution)/shard_map/ppermute | solution.py:17
  16.6 4.3 copy-start.6
  18.7 186.1 %all-gather.15.cloned.1.call-start = ((), (), s32[]{:S(2)}) async-start(), calls=%async_computation.1 | async-start | bytes 5242880 | tf_op jit(solution)/shard_map/all_gather | solution.py:135
  40.1 9.0 %copy-start.21 = (f32[256]{0:T(256)}, f32[256]{0:T(256)S(1)}, u32[]{:S(2)}) copy-start(f32[256]{0:T(256)S(1)} %fusion.82) | copy-start | bytes 3076
  77.4 11.7 %copy-start.30 = (f32[8]{0:T(128)S(1)}, f32[8]{0:T(128)}, u32[]{:S(2)}) copy-start(f32[8]{0:T(128)} %get-tuple-element.4) | copy-start | bytes 100
  89.2 34.9 %copy-start.17 = (pred[512,512]{0,1:T(8,128)(4,1)S(1)}, pred[512,512]{0,1:T(8,128)(4,1)}, u32[]{:S(2)}) copy-start(pred[512,512]{0,1:T(8,128)(4,1)} %iota_compare_fusion) | copy-start | bytes 786436
  124.1 9.8 %copy-start.19 = (f32[1,512,8]{1,2,0:T(8,128)S(1)}, f32[1,512,8]{1,2,0:T(8,128)}, u32[]{:S(2)}) copy-start(f32[1,512,8]{1,2,0:T(8,128)} %copy.68) | copy-start | bytes 49156
  124.1 9.8 %copy-start.20 = (f32[1,512,8]{1,2,0:T(8,128)S(1)}, f32[1,512,8]{1,2,0:T(8,128)}, u32[]{:S(2)}) copy-start(f32[1,512,8]{1,2,0:T(8,128)} %copy.69) | copy-start | bytes 49156
  124.1 11.1 %copy-start.25 = (f32[128]{0:T(128)S(1)}, f32[128]{0:T(128)}, u32[]{:S(2)}) copy-start(f32[128]{0:T(128)} %convert_reduce_fusion) | copy-start | bytes 1540
  124.1 29.3 %copy-start.27 = (s32[64]{0:T(128)S(1)}, s32[64]{0:T(128)}, u32[]{:S(2)}) copy-start(s32[64]{0:T(128)} %iota_add_fusion) | copy-start | bytes 772
  133.9 21.3 %copy-start.8 = (bf16[512,128]{1,0:T(8,128)(2,1)S(1)}, bf16[512,128]{1,0:T(8,128)(2,1)}, u32[]{:S(2)}) copy-start(bf16[512,128]{1,0:T(8,128)(2,1)} %param.7) | copy-start | bytes 393220
  161.1 3.2 copy-start.26
  164.3 8.5 %copy-start.12 = (f32[256,128]{1,0:T(8,128)}, f32[256,128]{1,0:T(8,128)S(1)}, u32[]{:S(2)}) copy-start(f32[256,128]{1,0:T(8,128)S(1)} %select_reduce_fusion.1) | copy-start | bytes 393220
  172.8 261.8 %copy-start.28 = (bf16[512,2048]{1,0:T(8,128)(2,1)S(1)}, bf16[512,2048]{1,0:T(8,128)(2,1)}, u32[]{:S(2)}) copy-start(bf16[512,2048]{1,0:T(8,128)(2,1)} %param.11) | copy-start | bytes 6291460
  172.8 261.7 %all-gather.17.cloned.1.call-start = ((), (), s32[]{:S(2)}) async-start(), calls=%async_computation.2 | async-start | bytes 18874368 | tf_op jit(solution)/shard_map/all_gather | solution.py:136
  173.6 334.4 %reduce-scatter.2.cloned.1.call-start = ((), (), s32[]{:S(2)}) async-start(), calls=%async_computation.3 | async-start | bytes 5242880 | tf_op jit(solution)/shard_map/reduce_scatter | solution.py:147
  464.5 158.1 %all-gather.21.cloned.1.call-start = ((), (), s32[]{:S(2)}) async-start(), calls=%async_computation.5 | async-start | bytes 1179648 | tf_op jit(solution)/shard_map/all_gather | solution.py:186
  509.5 2.3 copy-start.15
  509.5 2.8 copy-start.3
  512.3 3.8 copy-start.10
  516.1 24.8 %copy-start.16 = (f32[512,1,8]{0,2,1:T(8,128)S(1)}, f32[512,1,8]{0,2,1:T(8,128)}, u32[]{:S(2)}) copy-start(f32[512,1,8]{0,2,1:T(8,128)} %fusion.76) | copy-start | bytes 49156
  540.9 50.2 %copy-start.11 = (f32[512,8]{1,0:T(8,128)S(1)}, f32[512,8]{1,0:T(8,128)}, u32[]{:S(2)}) copy-start(f32[512,8]{1,0:T(8,128)} %copy.98) | copy-start | bytes 49156
  542.4 49.3 %copy-start.13 = (f32[256,128]{1,0:T(8,128)S(1)}, f32[256,128]{1,0:T(8,128)}, u32[]{:S(2)}) copy-start(f32[256,128]{1,0:T(8,128)} %copy-done.12) | copy-start | bytes 393220
  542.4 49.3 %copy-start.22 = (f32[256]{0:T(256)S(1)}, f32[256]{0:T(256)}, u32[]{:S(2)}) copy-start(f32[256]{0:T(256)} %copy-done.21) | copy-start | bytes 3076
  595.8 4.1 slice-start
  596.6 3.4 slice-start.1
  600.0 10.8 %copy-start.7 = (f32[16,512]{1,0:T(8,128)S(1)}, f32[16,512]{1,0:T(8,128)}, u32[]{:S(2)}) copy-start(f32[16,512]{1,0:T(8,128)} %copy-done.6) | copy-start | bytes 98308
  615.5 29.4 %copy-start.1 = (bf16[1,128,16]{1,2,0:T(8,128)(2,1)S(1)}, bf16[1,128,16]{1,2,0:T(8,128)(2,1)}, u32[]{:S(2)}) copy-start(bf16[1,128,16]{1,2,0:T(8,128)(2,1)} %param.9) | copy-start | bytes 12292
  (7 other events, 10.2 us)
Sparse Core Ops, SparseCore 0:
  18.8 40.0 all-gather.18
  173.0 31.7 all-gather.14
  206.9 227.6 all-gather.16
  464.6 43.3 reduce-scatter.1
  520.5 40.2 all-gather.20
where the time goes:
time: 660 us; the launch traced here: 653 us
  waiting for transfers between devices  264 us (40%)
  blocking collectives  213 us (32%)
  matrix products  119 us (18%)
  local copies, waits for them, and re-layouts  19.3 us (3%)
  between operations  16.9 us (3%)
  other arithmetic  14.9 us (2%)
    all_gather x1, waiting for transfers between devices, local(): proj_full = lax.all_gather(out_proj, 'ctx', axis=0, tiled=True)  230 us
    psum x1, blocking collectives, local(): lax.psum(jnp.sum(residual * residual), ('ctx', 'head')) / (total_rows * D)  39.3 us
    unnamed x2, blocking collectives  35.4 us
    all_gather x1, blocking collectives, local(): lax.all_gather(own_linear_v[None], 'ctx', axis=0, tiled=True)  31 us
    all_gather x1, waiting for transfers between devices, local(): all_heads = lax.all_gather(head_out, 'head', axis=1, tiled=True)  30.9 us
    all_gather x1, blocking collectives, local(): lax.all_gather(own_back_linear[None], 'ctx', axis=0, tiled=True)  30.8 us
    all_gather x1, blocking collectives, local(): lax.all_gather(own_den_square[None], 'ctx', axis=0, tiled=True)  20.5 us
    psum x1, blocking collectives, local(): feature_grad = lax.psum(own_grad, 'ctx')  20 us
  transfers between devices with their start and end apart: 6, of which 3 were waited for; matrix products, arithmetic and copies ran while one was open for 14% of the time, Pallas kernels for 0%

commit v1 on v0

--- a/solution.py
+++ b/solution.py
@@ -132,7 +132,12 @@
         .astype(jnp.bfloat16)
         .reshape(tok_rows, kv_groups * GROUP * HEAD_DIM)
     )
-    all_heads = lax.all_gather(head_out, "head", axis=1, tiled=True)
+    ring = [head_out]
+    for hop in range(3):
+        ring.append(lax.ppermute(ring[-1], "head", [(dev, (dev + 1) % 4) for dev in range(4)]))
+    all_heads = jnp.roll(
+        jnp.concatenate(ring[::-1], axis=1), (lax.axis_index("head") + 1) * ring[0].shape[1], axis=1
+    )
     proj_full = lax.all_gather(out_proj, "ctx", axis=0, tiled=True)
     projected = jnp.dot(all_heads, proj_full, preferred_element_type=jnp.float32)
     student_out = projected.astype(jnp.bfloat16)

time: 660 us -> 510 us (0.77)
  waiting for transfers between devices: 264 us -> 106 us
  local copies, waits for them, and re-layouts: 19.3 us -> 31.1 us
    all_gather x1, waiting for transfers between devices: 230 us -> 60.6 us  [local(): proj_full = lax.all_gather(out_proj, 'ctx', axis=0, tiled=True)]
    ppermute x0 -> x3, waiting for transfers between devices: none -> 43.1 us  [local(): lax.ppermute(ring[-1], 'head', [(dev, (dev + 1) % 4) for dev in range(4)])]
    all_gather x1 -> x0, waiting for transfers between devices: 30.9 us -> none  [local(): all_heads = lax.all_gather(head_out, 'head', axis=1, tiled=True)]
    unnamed x75 -> x82, local copies, waits for them, and re-layouts: 9.29 us -> 20.1 us
  transfers between devices with their start and end apart: 6 -> 8, of which waited for: 3 -> 5; matrix products, arithmetic and copies ran while one was open for 14% -> 21% of each run, Pallas kernels for 0% -> 0%
where the time goes in v1:
time: 510 us; the launch traced here: 502 us
  blocking collectives  214 us (42%)
  matrix products  114 us (22%)
  waiting for transfers between devices  106 us (21%)
  local copies, waits for them, and re-layouts  31.1 us (6%)
  between operations  17 us (3%)
  other arithmetic  15 us (3%)
  starting transfers between devices  5.6 us (1%)
    all_gather x1, waiting for transfers between devices, local(): proj_full = lax.all_gather(out_proj, 'ctx', axis=0, tiled=True)  60.6 us
    ppermute x3, waiting for transfers between devices, local(): lax.ppermute(ring[-1], 'head', [(dev, (dev + 1) % 4) for dev in range(4)])  43.1 us
    psum x1, blocking collectives, local(): lax.psum(jnp.sum(residual * residual), ('ctx', 'head')) / (total_rows * D)  39.3 us
    unnamed x2, blocking collectives  35.7 us
    all_gather x1, blocking collectives, local(): lax.all_gather(own_linear_v[None], 'ctx', axis=0, tiled=True)  31.1 us
    all_gather x1, blocking collectives, local(): lax.all_gather(own_back_linear[None], 'ctx', axis=0, tiled=True)  30.7 us
    all_gather x1, blocking collectives, local(): lax.all_gather(own_den_square[None], 'ctx', axis=0, tiled=True)  20.6 us
    unnamed x82, local copies, waits for them, and re-layouts  20.1 us
  transfers between devices with their start and end apart: 8, of which 5 were waited for; matrix products, arithmetic and copies ran while one was open for 21% of the time, Pallas kernels for 0%

profile of v1, /device:TPU:0, one launch (start us, length us, event | category | flops | bytes accessed | tf_op | source)
XLA Modules:
  0.0 502.2 jit_solution(14417146907601765747)
XLA Ops:
  14.0 5.4 %collective-permute-start = (bf16[2,64,128]{2,1,0:T(8,128)(2,1)}, bf16[2,64,128]{2,1,0:T(8,128)(2,1)}, u32[]{:S(2)}, u32[]{:S(2)}) collective-permute-start(bf16[2,64,128]{2,1,0:T(8,128)(2,1)} %pad_maximum_fusion.2), channel_id=1, source_target_pairs={{0,4},{4,8},{8,12},{12,16},{16,20},{20,24},{24,28},{1,5},{5,9},{9,... | collective-permute-start | bytes 98312 | tf_op jit(solution)/shard_map/ppermute | solution.py:17
  19.5 18.1 %all_gather.36 = f32[8,1,256]{2,1,0:T(1,128)S(1)} all-gather(f32[1,1,256]{2,1,0:T(1,128)S(1)} %broadcast_in_dim.148), channel_id=1, replica_groups=mesh['ctx'=8,'head'=4] {'ctx'}, dimensions={0}, use_global_device_ids=true | all-gather | bytes 9216 | tf_op jit(solution)/shard_map/all_gather | solution.py:109
  40.8 7.1 %fusion.114 = f32[1,512,8]{0,1,2:T(8,128)S(1)} fusion(f32[256,1,1]{0,1,2:T(1,128)S(1)} %bitcast.399, f32[512,8,256]{0,2,1:T(8,128)S(1)} %bitcast.366), kind=kOutput, calls=%fused_computation.179 | convolution fusion | flops 12582912 | bytes 4211712 | tf_op jit(solution)/shard_map/tgqk,gk->tgq/dot_general | solution.py:125
  51.4 18.4 %all-reduce.3 = (f32[128]{0:T(128)S(1)}, f32[8]{0:T(128)}) all-reduce(f32[128]{0:T(128)S(1)} %dynamic-update-slice, f32[8]{0:T(128)S(1)} %dynamic-update-slice.1), channel_id=5, replica_groups=mesh['ctx'=8,'head'=4] {'ctx'}, use_global_device_ids=true, to_apply=%add | all-reduce | flops 136 | bytes 1088
  70.0 3.4 fusion.94
  74.7 18.1 %all-gather.8 = f32[8,1,128]{2,1,0:T(1,128)S(1)} all-gather(f32[1,1,128]{2,1,0:T(1,128)S(1)} %bitcast.400), channel_id=4, replica_groups=mesh['ctx'=8,'head'=4] {'ctx'}, dimensions={0}, use_global_device_ids=true | all-gather | bytes 4608 | tf_op jit(solution)/shard_map/all_gather | solution.py:108
  93.8 31.1 %all-gather.1 = f32[128,128]{1,0:T(8,128)S(1)} all-gather(f32[16,128]{1,0:T(8,128)S(1)} %fusion.99), channel_id=3, replica_groups=mesh['ctx'=8,'head'=4] {'ctx'}, dimensions={0}, use_global_device_ids=true | all-gather | bytes 73728 | tf_op jit(solution)/shard_map/all_gather | solution.py:107
  126.4 9.4 %fusion.7 = (f32[8,512]{1,0:T(8,128)S(1)}, f32[512,512,8]{1,0,2:T(8,128)S(1)}) fusion(pred[512,512]{0,1:T(8,128)(4,1)S(1)} %iota_compare_fusion, f32[512,8,16]{0,2,1:T(8,128)S(1)} %convolution_bitcast_fusion.2, f32[16,512]{1,0:T(8,128)} %copy-done.6), kind=kOutput, calls=%fused_computation.10 | convolution fusion | flops 417329152 | bytes 8962048 | tf_op jit(solution)/shard_map/tgqf,sgf->gqts/dot_general | solution.py:93
  137.8 3.1 fusion.85
  141.0 6.2 %fusion.5 = f32[8,512,128]{1,2,0:T(8,128)} fusion(f32[512,512,8]{1,0,2:T(8,128)S(1)} %get-tuple-element.13, pred[512,512]{0,1:T(8,128)(4,1)S(1)} %iota_compare_fusion, bf16[512,128]{1,0:T(8,128)(2,1)S(1)} %copy-done.5), kind=kOutput, calls=%fused_computation.7 | convolution fusion | flops 3233808384 | bytes 10878976 | tf_op jit(solution)/shard_map/gqts,sge->tgqe/dot_general | solution.py:96
  151.0 2.6 convolution_bitcast_fusion
  158.0 8.3 %add_convert_fusion = (bf16[512,1,8,128]{0,3,2,1:T(8,128)(2,1)S(1)}, f32[512,1,8,128]{0,3,2,1:T(8,128)}) fusion(f32[512,1,8,128]{0,3,2,1:T(8,128)} %copy.53, f32[512,8]{0,1:T(8,128)} %bitcast.391, f32[128]{0:T(128)S(1)} %copy-done.26, f32[128,512,8]{1,0,2:T(8,128)} %fusion.85, f32[512,8,256]{0,2,1:T(8,128)} %bitcast.367, ...), kind=kOutput, calls=%fused_computation.40 | convolution fusion | flops 1614807040 | bytes 13779456 | tf_op jit(solution)/shard_map/tgqk,gke->tgqe/dot_general | solution.py:119
  166.3 14.2 %collective-permute-done.1 = bf16[512,1024]{0,1:T(8,128)(2,1)S(1)} collective-permute-done((bf16[512,1024]{0,1:T(8,128)(2,1)S(1)}, bf16[512,1024]{0,1:T(8,128)(2,1)S(1)}, u32[]{:S(2)}, u32[]{:S(2)}) %collective-permute-start.1) | collective-permute-done | bytes 1048608 | tf_op jit(solution)/shard_map/ppermute | solution.py:137
  180.5 14.3 %collective-permute-done.2 = bf16[512,1024]{0,1:T(8,128)(2,1)} collective-permute-done((bf16[512,1024]{0,1:T(8,128)(2,1)S(1)}, bf16[512,1024]{0,1:T(8,128)(2,1)}, u32[]{:S(2)}, u32[]{:S(2)}) %collective-permute-start.2) | collective-permute-done | bytes 1048608 | tf_op jit(solution)/shard_map/ppermute | solution.py:137
  194.8 14.5 %collective-permute-done.3 = bf16[512,1024]{0,1:T(8,128)(2,1)} collective-permute-done((bf16[512,1024]{0,1:T(8,128)(2,1)}, bf16[512,1024]{0,1:T(8,128)(2,1)}, u32[]{:S(2)}, u32[]{:S(2)}) %collective-permute-start.3) | collective-permute-done | bytes 1048608 | tf_op jit(solution)/shard_map/ppermute | solution.py:137
  209.4 2.4 constant_dynamic-update-slice_fusion.7
  216.1 2.3 constant_dynamic-update-slice_fusion.3
  222.8 60.6 %all-gather.14.cloned.1.call-done = bf16[4096,2048]{1,0:T(8,128)(2,1)} async-done(((bf16[512,2048]{1,0:T(8,128)(2,1)}), bf16[4096,2048]{1,0:T(8,128)(2,1)}) %all-gather.14.cloned.1.call-update) | async-done | bytes 16777232 | tf_op jit(solution)/shard_map/all_gather | solution.py:141
  283.3 15.3 %multiply_reduce_fusion.2 = (f32[]{:T(128)}, bf16[512,2048]{1,0:T(8,128)(2,1)S(1)}) fusion(bf16[512,2048]{1,0:T(8,128)(2,1)} %param.11, bf16[4096,2048]{1,0:T(8,128)(2,1)} %all-gather.14.cloned.1.call-done, bf16[512,8192]{0,1:T(8,128)(2,1)} %constant_dynamic-update-slice_fusion, s32[]{:T(128)S(6)} %select_n.73), kind=kOutput, calls=%fused_computation.16 | convolution fusion | flops 8596226048 | bytes 25165832 | tf_op jit(solution)/shard_map/dot_general | solution.py:142
  299.9 13.8 %convolution_convert_fusion = bf16[512,4096]{1,0:T(8,128)(2,1)} fusion(bf16[4096,2048]{1,0:T(8,128)(2,1)} %all-gather.14.cloned.1.call-done, bf16[512,2048]{1,0:T(8,128)(2,1)S(1)} %copy-done.27, bf16[512,2048]{1,0:T(8,128)(2,1)S(1)} %get-tuple-element.21), kind=kOutput, calls=%fused_computation.9 | convolution fusion | flops 8597274624 | bytes 25165824 | tf_op jit(solution)/shard_map/dot_general | solution.py:148
  315.3 39.3 %psum.14 = f32[]{:T(128)} all-reduce(f32[]{:T(128)} %get-tuple-element.20), channel_id=1, replica_groups=mesh['ctx'=8,'head'=4] {'ctx','head'}, use_global_device_ids=true, to_apply=%region_13.14 | all-reduce | flops 1 | bytes 8 | tf_op jit(solution)/shard_map/psum | solution.py:146
  358.8 2.3 multiply_reduce_fusion.3
  361.8 3.3 convolution_bitcast_fusion.7
  365.6 4.2 convolution_bitcast_fusion.3
  369.9 20.6 %all-gather.9 = f32[8,1,256]{2,1,0:T(1,128)S(1)} all-gather(f32[1,1,256]{2,1,0:T(1,128)S(1)} %convolution_bitcast_fusion.7), channel_id=9, replica_groups=mesh['ctx'=8,'head'=4] {'ctx'}, dimensions={0}, use_global_device_ids=true | all-gather | bytes 9216 | tf_op jit(solution)/shard_map/all_gather | solution.py:193
  392.0 30.7 %all-gather.4 = f32[128,128]{1,0:T(8,128)S(1)} all-gather(f32[16,128]{1,0:T(8,128)S(1)} %convolution_bitcast_fusion.6), channel_id=6, replica_groups=mesh['ctx'=8,'head'=4] {'ctx'}, dimensions={0}, use_global_device_ids=true | all-gather | bytes 73728 | tf_op jit(solution)/shard_map/all_gather | solution.py:192
  423.1 17.3 %all-reduce.2 = f32[128]{0:T(128)S(1)} all-reduce(f32[128]{0:T(128)S(1)} %dynamic-update-slice.2), channel_id=7, replica_groups=mesh['ctx'=8,'head'=4] {'ctx'}, use_global_device_ids=true, to_apply=%add.2 | all-reduce | flops 128 | bytes 1024
  441.2 4.1 fusion.9
  449.5 10.8 %fusion.3 = f32[8,512,512]{1,2,0:T(8,128)S(1)} fusion(f32[512,512,8]{1,0,2:T(8,128)S(1)} %bitcast.402, f32[8,512]{1,0:T(8,128)S(1)} %get-tuple-element.7, pred[512,512]{0,1:T(8,128)(4,1)S(1)} %copy-done.19, bf16[512,128]{1,0:T(8,128)(2,1)S(1)} %copy-done.5, f32[64,8,8,128]{3,2,1,0:T(8,128)S(1)} %bitcast.381, bf16[512,1024]{1,0:T(8,128)(2,1)S(1)} %copy-done.11), kind=kOutput, calls=%fused_computation.4 | convolution fusion | flops 3234856960 | bytes 20332544 | tf_op jit(solution)/shard_map/tgqe,sge->gqts/dot_general | solution.py:159
  460.3 4.0 fusion.36
  465.0 7.1 %convolution_bitcast_fusion.4 = f32[512,1,16]{0,2,1:T(8,128)S(1)} fusion(f32[512,8,16]{0,2,1:T(8,128)S(1)} %convolution_bitcast_fusion.2, f32[8,512,512]{1,2,0:T(8,128)S(1)} %fusion.3), kind=kOutput, calls=%fused_computation.67 | convolution fusion | flops 402653184 | bytes 8683520 | tf_op jit(solution)/shard_map/gqts,tgqf->sgf/dot_general | solution.py:164
  474.4 20.0 %psum.15 = f32[1,128,16]{1,2,0:T(8,128)} all-reduce(f32[1,128,16]{1,2,0:T(8,128)S(1)} %fusion.51), channel_id=1, replica_groups=mesh['ctx'=8,'head'=4] {'ctx'}, use_global_device_ids=true, to_apply=%region_20.21 | all-reduce | flops 2048 | bytes 16384 | tf_op jit(solution)/shard_map/psum | solution.py:215
  (149 shorter events, 52.7 us)
Async XLA Ops:
  7.2 30.5 %copy-start.4 = (bf16[512,1024]{1,0:T(8,128)(2,1)S(1)}, bf16[512,1024]{1,0:T(8,128)(2,1)}, u32[]{:S(2)}) copy-start(bf16[512,1024]{1,0:T(8,128)(2,1)} %param.6) | copy-start | bytes 3145732
  7.2 149.4 %all-gather.16.cloned.1.call-start = ((), (), s32[]{:S(2)}) async-start(), calls=%async_computation.3 | async-start | bytes 1179648 | tf_op jit(solution)/shard_map/all_gather | solution.py:106
  9.0 28.6 %copy-start.6 = (f32[16,512]{1,0:T(8,128)}, f32[16,512]{1,0:T(8,128)S(1)}, u32[]{:S(2)}) copy-start(f32[16,512]{1,0:T(8,128)S(1)} %get-tuple-element.15) | copy-start | bytes 98308
  11.1 272.2 %all-gather.14.cloned.1.call-start = ((), (), s32[]{:S(2)}) async-start(), calls=%async_computation.1 | async-start | bytes 18874368 | tf_op jit(solution)/shard_map/all_gather | solution.py:141
  11.9 345.5 %reduce-scatter.2.cloned.1.call-start = ((), (), s32[]{:S(2)}) async-start(), calls=%async_computation.2 | async-start | bytes 5242880 | tf_op jit(solution)/shard_map/reduce_scatter | solution.py:152
  14.0 134.1 %collective-permute-start = (bf16[2,64,128]{2,1,0:T(8,128)(2,1)}, bf16[2,64,128]{2,1,0:T(8,128)(2,1)}, u32[]{:S(2)}, u32[]{:S(2)}) collective-permute-start(bf16[2,64,128]{2,1,0:T(8,128)(2,1)} %pad_maximum_fusion.2), channel_id=1, source_target_pairs={{0,4},{4,8},{8,12},{12,16},{16,20},{20,24},{24,28},{1,5},{5,9},{9,... | collective-permute-start | bytes 98312 | tf_op jit(solution)/shard_map/ppermute | solution.py:17
  40.8 8.4 %copy-start.29 = (u32[32]{0:T(128)S(1)}, u32[32]{0:T(128)}, u32[]{:S(2)}) copy-start(u32[32]{0:T(128)} %constant.94) | copy-start | bytes 388
  47.9 26.8 %copy-start.5 = (bf16[512,128]{1,0:T(8,128)(2,1)S(1)}, bf16[512,128]{1,0:T(8,128)(2,1)}, u32[]{:S(2)}) copy-start(bf16[512,128]{1,0:T(8,128)(2,1)} %param.8) | copy-start | bytes 393220
  70.0 56.3 %copy-start.24 = (f32[16]{0:T(128)}, f32[16]{0:T(128)S(1)}, u32[]{:S(2)}) copy-start(f32[16]{0:T(128)S(1)} %select_reduce_fusion.5) | copy-start | bytes 196
  126.4 14.6 %copy-start.18 = (pred[512,512]{0,1:T(8,128)(4,1)}, pred[512,512]{0,1:T(8,128)(4,1)S(1)}, u32[]{:S(2)}) copy-start(pred[512,512]{0,1:T(8,128)(4,1)S(1)} %iota_compare_fusion) | copy-start | bytes 786436
  126.4 9.5 %copy-start.20 = (f32[1,512,8]{1,2,0:T(8,128)S(1)}, f32[1,512,8]{1,2,0:T(8,128)}, u32[]{:S(2)}) copy-start(f32[1,512,8]{1,2,0:T(8,128)} %copy.68) | copy-start | bytes 49156
  126.4 9.5 %copy-start.21 = (f32[1,512,8]{1,2,0:T(8,128)S(1)}, f32[1,512,8]{1,2,0:T(8,128)}, u32[]{:S(2)}) copy-start(f32[1,512,8]{1,2,0:T(8,128)} %copy.69) | copy-start | bytes 49156
  135.9 11.3 %copy-start.30 = (f32[512,512,8]{1,0,2:T(8,128)}, f32[512,512,8]{1,0,2:T(8,128)S(1)}, u32[]{:S(2)}) copy-start(f32[512,512,8]{1,0,2:T(8,128)S(1)} %get-tuple-element.13) | copy-start | bytes 25165828
  141.0 7.9 %copy-start.8 = (bf16[512,128]{1,0:T(8,128)(2,1)S(1)}, bf16[512,128]{1,0:T(8,128)(2,1)}, u32[]{:S(2)}) copy-start(bf16[512,128]{1,0:T(8,128)(2,1)} %param.7) | copy-start | bytes 393220
  153.6 4.4 copy-start.26
  158.0 8.3 %copy-start.13 = (f32[256,128]{1,0:T(8,128)}, f32[256,128]{1,0:T(8,128)S(1)}, u32[]{:S(2)}) copy-start(f32[256,128]{1,0:T(8,128)S(1)} %select_reduce_fusion.1) | copy-start | bytes 393220
  166.3 14.2 %collective-permute-start.1 = (bf16[512,1024]{0,1:T(8,128)(2,1)S(1)}, bf16[512,1024]{0,1:T(8,128)(2,1)S(1)}, u32[]{:S(2)}, u32[]{:S(2)}) collective-permute-start(bf16[512,1024]{0,1:T(8,128)(2,1)S(1)} %bitcast.373), channel_id=1, source_target_pairs={{0,1},{1,2},{2,3},{3,0},{4,5},{5,6},{6,7},{7,4},{8,9},{9,10},{10,1... | collective-permute-start | bytes 3145736 | tf_op jit(solution)/shard_map/ppermute | solution.py:137
  180.5 14.3 %collective-permute-start.2 = (bf16[512,1024]{0,1:T(8,128)(2,1)S(1)}, bf16[512,1024]{0,1:T(8,128)(2,1)}, u32[]{:S(2)}, u32[]{:S(2)}) collective-permute-start(bf16[512,1024]{0,1:T(8,128)(2,1)S(1)} %collective-permute-done.1), channel_id=1, source_target_pairs={{0,1},{1,2},{2,3},{3,0},{4,5},{5,6},{6,7},{7,4},{8,9},{9,10},{10,1... | collective-permute-start | bytes 3145736 | tf_op jit(solution)/shard_map/ppermute | solution.py:137
  194.8 14.5 %collective-permute-start.3 = (bf16[512,1024]{0,1:T(8,128)(2,1)}, bf16[512,1024]{0,1:T(8,128)(2,1)}, u32[]{:S(2)}, u32[]{:S(2)}) collective-permute-start(bf16[512,1024]{0,1:T(8,128)(2,1)} %collective-permute-done.2), channel_id=1, source_target_pairs={{0,1},{1,2},{2,3},{3,0},{4,5},{5,6},{6,7},{7,4},{8,9},{9,10},{10,1... | collective-permute-start | bytes 3145736 | tf_op jit(solution)/shard_map/ppermute | solution.py:137
  222.8 77.1 %copy-start.27 = (bf16[512,2048]{1,0:T(8,128)(2,1)S(1)}, bf16[512,2048]{1,0:T(8,128)(2,1)}, u32[]{:S(2)}) copy-start(bf16[512,2048]{1,0:T(8,128)(2,1)} %param.11) | copy-start | bytes 6291460
  313.8 158.3 %all-gather.18.cloned.1.call-start = ((), (), s32[]{:S(2)}) async-start(), calls=%async_computation.4 | async-start | bytes 1179648 | tf_op jit(solution)/shard_map/all_gather | solution.py:191
  358.8 6.8 %copy-start.10 = (bf16[512,1024]{1,0:T(8,128)(2,1)S(1)}, bf16[512,1024]{1,0:T(8,128)(2,1)}, u32[]{:S(2)}) copy-start(bf16[512,1024]{1,0:T(8,128)(2,1)} %reduce-scatter.2.cloned.1.call-done) | copy-start | bytes 3145732
  358.8 6.8 %copy-start.16 = (f32[512,1,8]{0,2,1:T(8,128)S(1)}, f32[512,1,8]{0,2,1:T(8,128)}, u32[]{:S(2)}) copy-start(f32[512,1,8]{0,2,1:T(8,128)} %fusion.81) | copy-start | bytes 49156
  365.6 24.9 %copy-start.11 = (bf16[512,1024]{1,0:T(8,128)(2,1)S(1)}, bf16[512,1024]{1,0:T(8,128)(2,1)}, u32[]{:S(2)}) copy-start(bf16[512,1024]{1,0:T(8,128)(2,1)} %reduce-scatter.2.cloned.1.call-done) | copy-start | bytes 3145732
  365.6 24.9 %copy-start.17 = (f32[512,1,8]{0,2,1:T(8,128)S(1)}, f32[512,1,8]{0,2,1:T(8,128)}, u32[]{:S(2)}) copy-start(f32[512,1,8]{0,2,1:T(8,128)} %fusion.81) | copy-start | bytes 49156
  369.9 70.7 %copy-start.12 = (f32[512,8]{1,0:T(8,128)S(1)}, f32[512,8]{1,0:T(8,128)}, u32[]{:S(2)}) copy-start(f32[512,8]{1,0:T(8,128)} %copy.98) | copy-start | bytes 49156
  390.5 50.6 %copy-start.14 = (f32[256,128]{1,0:T(8,128)S(1)}, f32[256,128]{1,0:T(8,128)}, u32[]{:S(2)}) copy-start(f32[256,128]{1,0:T(8,128)} %copy-done.13) | copy-start | bytes 393220
  390.5 50.6 %copy-start.23 = (f32[256]{0:T(256)S(1)}, f32[256]{0:T(256)}, u32[]{:S(2)}) copy-start(f32[256]{0:T(256)} %copy-done.22) | copy-start | bytes 3076
  445.3 4.1 slice-start
  449.5 10.8 %copy-start.7 = (f32[16,512]{1,0:T(8,128)S(1)}, f32[16,512]{1,0:T(8,128)}, u32[]{:S(2)}) copy-start(f32[16,512]{1,0:T(8,128)} %copy-done.6) | copy-start | bytes 98308
  464.3 30.0 %copy-start.1 = (bf16[1,128,16]{1,2,0:T(8,128)(2,1)S(1)}, bf16[1,128,16]{1,2,0:T(8,128)(2,1)}, u32[]{:S(2)}) copy-start(bf16[1,128,16]{1,2,0:T(8,128)(2,1)} %param.9) | copy-start | bytes 12292
  465.0 9.2 %copy-start.9 = (bf16[512,128]{1,0:T(8,128)(2,1)S(1)}, bf16[512,128]{1,0:T(8,128)(2,1)}, u32[]{:S(2)}) copy-start(bf16[512,128]{1,0:T(8,128)(2,1)} %param.7) | copy-start | bytes 393220
  (9 other events, 16.4 us)
Sparse Core Ops, SparseCore 0:
  11.2 42.9 all-gather.15
  56.4 226.8 all-gather.13
  313.9 43.3 reduce-scatter.1
  370.0 40.2 all-gather.17
